TPU v7x, 256 devices: a whole 4x4x8 slice. The times are simulated.
256 devices in a mesh: pipe: 32 (over z, y), expert: 8 (over x, core).
Axes of the slice: x: 4, y: 4, z: 8, core: 2. Of those that a mesh axis runs over, the one named last changes fastest.
Arguments:
- saved: bfloat16 [2, 1024, 6144], P(None, 'expert', 'pipe'), may hold values from -6 to 6
- top_grad: bfloat16 [2, 1024, 6144], P(None, 'expert', 'pipe'), may hold values from -6 to 6
- norm_gain: float32 [6144], P('pipe'), may hold values from 0.1 to 1.9
- w_gate: bfloat16 [8, 6144, 8192], P('expert', None, 'pipe'), may hold values from -0.078125 to 0.078125
- w_up: bfloat16 [8, 6144, 8192], P('expert', None, 'pipe'), may hold values from -0.078125 to 0.078125
- w_down: bfloat16 [8, 8192, 6144], P('expert', 'pipe'), may hold values from -0.0625 to 0.0625
- routes: int32 [2, 1024, 2], P(None, 'expert'), may hold values from 0 to 7, all different within a row; in each aligned block of 128 rows (0 to 127, 128 to 255, ..., all dimensions but the last counted through in order) at most 48 rows name the same one
- gates: float32 [2, 1024, 2], P(None, 'expert'), may hold values from 0.1 to 0.9
Outputs:
- input_grads: float32 [2, 1024, 6144], P(None, 'expert', 'pipe')
- grad_gain: float32 [6144], P('pipe')
Inputs may be any that keep to these rules, and one draw needn't show every extreme that they name: `routes`: each token names two different experts; in every aligned block of 128 rows of one micro-batch no expert is named more than 48 times, a bound that some block reaches.
All inputs are finite; a program needn't handle non-finite values.
Results may differ from a plain program's by a relative error of at most 0.017.
Values may be sent and summed in bfloat16 or wider, within the bound.
No kernel may reach another device: no remote copies, remote signals or barrier semaphores. Data moves between devices by JAX's collectives and lax.ppermute only.
A program may use at most 128 MiB of HBM per device.

v0:
```python
import jax
import jax.numpy as jnp
from jax import lax
from jax.sharding import Mesh
from jax.sharding import PartitionSpec as P

PIPE = ("pipe_0", "pipe_1")
eps = 1e-05


def from_everyone(x, axis):
    devices = lax.axis_size(axis)
    return lax.all_to_all(jnp.broadcast_to(x[None], (devices, *x.shape)), axis, 0, 0, tiled=True)


def taken_together(x, axis):
    everything = from_everyone(x, axis)
    return jnp.sum(everything, axis=0)


def in_one_piece(arrays, axis, split_dim, concat_dim, along):
    ends, at = ([], 0)
    for a in arrays[:-1]:
        at += a.shape[along]
        ends.append(at)
    both = jnp.concatenate(arrays, axis=along)
    return tuple(
        jnp.split(
            lax.all_to_all(both, axis, split_axis=split_dim, concat_axis=concat_dim, tiled=True),
            ends,
            axis=along,
        )
    )


def rows_first(arrays, axis, dims):
    turned = [jnp.moveaxis(a, dim, 0) for a, dim in zip(arrays, dims)]
    both = jnp.concatenate([t.reshape(len(t), -1) for t in turned], axis=1)
    out, at, gathered = (lax.all_gather(both, axis, axis=0, tiled=True), 0, [])
    for t, dim in zip(turned, dims):
        section = out[:, at : at + t[0].size].reshape(-1, *t.shape[1:])
        gathered.append(jnp.moveaxis(section, 0, dim))
        at += t[0].size
    return tuple(gathered)


def sum_by_axis(terms, axes):
    total = terms.astype(jnp.bfloat16)
    for axis in axes:
        total = lax.psum_scatter(total, axis, scatter_dimension=0, tiled=True)
    return total.astype(jnp.float32)


def slot_matrix(route_block, n_experts, capacity):
    flat = route_block.reshape(-1)
    onehot = (flat[:, None] == jnp.arange(n_experts, dtype=jnp.int32)[None, :]).astype(jnp.int32)
    before = jnp.cumsum(onehot, axis=0) - onehot
    slot = jnp.sum(before * onehot, axis=1)
    target = flat * capacity + slot
    return (target[None, :] == jnp.arange(n_experts * capacity, dtype=jnp.int32)[:, None]).astype(
        jnp.bfloat16
    )


def contract_last(left, right):
    return lax.dot_general(
        left, right, (((1,), (1,)), ((), ())), preferred_element_type=jnp.float32
    )


def body(saved, top_grad, norm_gain, w_gate, w_up, w_down, routes, gates):
    n_pipe = lax.axis_size(PIPE)
    n_experts = lax.axis_size("expert")
    micro, tok, part = saved.shape
    width = part * n_pipe
    capacity = 3 * tok // n_experts
    slots = n_experts * capacity
    wg = w_gate[0]
    wu = w_up[0]
    down_weight = w_down[0]
    hidden_width = wg.shape[1]
    inputs = saved.astype(jnp.float32)
    upstream = top_grad.astype(jnp.float32)
    squares = taken_together(jnp.sum(inputs * inputs, axis=-1), PIPE)
    scale = lax.rsqrt(squares / width + eps)[:, :, None]
    normed = (inputs * scale * norm_gain).astype(jnp.bfloat16)
    placing = jax.vmap(lambda block: slot_matrix(block, n_experts, capacity))(routes)
    pair_grad = (
        (gates[:, :, :, None] * upstream[:, :, None, :])
        .reshape(micro, 2 * tok, part)
        .astype(jnp.bfloat16)
    )
    sent_x = jnp.einsum(
        "msp,mpd->msd", placing, jnp.repeat(normed, 2, axis=1), preferred_element_type=jnp.float32
    ).astype(jnp.bfloat16)
    sent_g = jnp.einsum(
        "msp,mpd->msd", placing, pair_grad, preferred_element_type=jnp.float32
    ).astype(jnp.bfloat16)
    got_x, got_g = in_one_piece((sent_x, sent_g), "expert", 1, 1, 0)
    input_slice, gradient_slice = rows_first((got_x, got_g), PIPE, (2, 2))
    gate_weight_rows = wg
    up_weight_rows = wu
    gate_partial_total = jnp.einsum(
        "wsk,kz->wsz", input_slice, gate_weight_rows, preferred_element_type=jnp.float32
    )
    up_partial_total = jnp.einsum(
        "wsk,kz->wsz", input_slice, up_weight_rows, preferred_element_type=jnp.float32
    )
    hidden_partial_total = jnp.einsum(
        "vun,zn->vuz", gradient_slice, down_weight, preferred_element_type=jnp.float32
    )
    sig = jax.nn.sigmoid(gate_partial_total)
    act = gate_partial_total * sig
    d_a = (
        hidden_partial_total * up_partial_total * sig * (1.0 + gate_partial_total * (1.0 - sig))
    ).astype(jnp.bfloat16)
    d_b = (hidden_partial_total * act).astype(jnp.bfloat16)
    flat_a = d_a.reshape(micro * slots, hidden_width)
    flat_b = d_b.reshape(micro * slots, hidden_width)
    gate_weight_rows = wg
    up_weight_rows = wu
    summed = sum_by_axis(
        contract_last(gate_weight_rows, flat_a) + contract_last(up_weight_rows, flat_b), PIPE
    )
    d_rows = summed.astype(jnp.bfloat16).reshape(part, micro, slots)
    returned = lax.all_to_all(d_rows, "expert", split_axis=2, concat_axis=2, tiled=True)
    d_pairs = jnp.einsum("dms,msp->mpd", returned, placing, preferred_element_type=jnp.float32)
    d_norm = d_pairs.reshape(micro, tok, 2, part).sum(axis=2)
    scaled = norm_gain * d_norm
    inner = taken_together(jnp.sum(scaled * inputs, axis=-1), PIPE)
    d_x = scale * scaled - inputs * scale**3 * (inner / width)[:, :, None]
    input_grads = upstream + d_x
    gain_part = jnp.sum(d_norm * inputs * scale, axis=(0, 1))
    grad_gain = taken_together(gain_part, "expert")
    return (input_grads, grad_gain)


def solution(mesh):
    torus = Mesh(mesh.devices.reshape(8, 4, mesh.shape["expert"]), ("pipe_0", "pipe_1", "expert"))
    in_specs = (
        P(None, "expert", PIPE),
        P(None, "expert", PIPE),
        P(PIPE),
        P("expert", None, PIPE),
        P("expert", None, PIPE),
        P("expert", PIPE, None),
        P(None, "expert", None),
        P(None, "expert", None),
    )
    out_specs = (P(None, "expert", PIPE), P(PIPE))
    return jax.shard_map(body, mesh=torus, in_specs=in_specs, out_specs=out_specs, check_vma=False)
```

profile of v0, /device:TPU:1, one launch (start us, length us, event | category | flops | bytes accessed | tf_op | source)
XLA Modules:
  0.0 480.7 jit_solution(8491837674366570736)
XLA Ops:
  7.2 1.2 copy.84
  8.4 0.2 fusion.28
  8.6 0.6 broadcast_in_dim.8
  9.3 12.2 %all-to-all-start = ((f32[32,2,128]{2,1,0:T(2,128)}), f32[32,2,128]{2,1,0:T(2,128)}, u32[]{:S(2)}, u32[]{:S(2)}) async-start(f32[32,2,128]{2,1,0:T(2,128)} %broadcast_in_dim.8), calls=%async_computation | async-start | bytes 65536 | tf_op jit(solution)/shard_map/all_to_all | solution.py:13
  21.5 0.8 copy.88
  22.3 0.1 eq.39
  22.5 0.1 reshape.84
  22.6 1.2 reduce-window.6
  23.8 0.2 slice_reduce_fusion
  24.1 1.0 copy.83
  25.2 0.8 convert_element_type.40
  26.0 0.8 copy.108
  26.8 1.3 fusion.23
  28.1 1.1 convolution_convert_fusion
  29.1 1.0 all-to-all-done
  30.1 0.8 reduce_sum.73
  31.1 0.9 fusion.30
  32.0 0.1 broadcast_in_dim.9
  32.1 0.3 convolution_convert_fusion.1
  32.5 1.8 pad_maximum_fusion
  34.3 2.2 copy.94
  36.5 18.5 %all_to_all.26 = bf16[4,384,192]{2,0,1:T(4,128)(2,1)S(1)} all-to-all(bf16[4,384,192]{2,0,1:T(4,128)(2,1)} %copy.94), channel_id=1, replica_groups=mesh['pipe_0'=8,'pipe_1'=4,'expert'=8] {'expert'}, dimensions={1} | all-to-all | bytes 1179648 | tf_op jit(solution)/shard_map/all_to_all | solution.py:29
  55.0 1.4 slice_bitcast_fusion.1
  56.5 2.0 copy.95
  58.5 1.7 copy.115
  60.2 2.0 copy.96
  62.2 1.0 copy.116
  63.1 1.8 pad_maximum_fusion.1
  65.0 0.2 reduce-scatter.5.cloned.1.call-start
  65.2 147.0 %all-gather.2.cloned.1.call-done = bf16[6144,1536]{1,0:T(8,128)(2,1)} async-done(((bf16[192,1536]{1,0:T(8,128)(2,1)}), bf16[6144,1536]{1,0:T(8,128)(2,1)}) %all-gather.2.cloned.1.call-update) | async-done | bytes 18874384 | tf_op jit(solution)/shard_map/all_gather | solution.py:39
  212.3 14.5 %fusion.42 = (bf16[6144,768]{1,0:T(8,128)(2,1)}, bf16[6144,768]{1,0:T(8,128)(2,1)}) fusion(bf16[6144,1536]{1,0:T(8,128)(2,1)} %all-gather.2.cloned.1.call-done), kind=kLoop, calls=%fused_computation.59 | loop fusion | bytes 37748736 | tf_op jit(solution)/shard_map/slice | solution.py:41
  226.8 12.7 %copy.98 = bf16[6144,768]{0,1:T(8,128)(2,1)} copy(bf16[6144,768]{1,0:T(8,128)(2,1)} %get-tuple-element.12) | data formatting | bytes 18874368 | tf_op jit(solution)/shard_map/slice | solution.py:41
  239.5 12.7 %copy.97 = bf16[6144,768]{0,1:T(8,128)(2,1)} copy(bf16[6144,768]{1,0:T(8,128)(2,1)} %get-tuple-element.13) | data formatting | bytes 18874368 | tf_op jit(solution)/shard_map/slice | solution.py:41
  252.3 5.3 %fusion.1 = f32[2,384,256]{2,1,0:T(8,128)S(1)} fusion(bf16[2,384,6144]{2,1,0:T(8,128)(2,1)} %bitcast.67, bf16[1,6144,256]{2,1,0:T(8,128)(2,1)S(1)} %copy-done), kind=kOutput, calls=%fused_computation.2 | convolution fusion | flops 2415919104 | bytes 13369344 | tf_op jit(solution)/shard_map/wsk,kz->wsz/dot_general | solution.py:103
  257.6 1.1 copy-done.1
  258.7 0.9 copy-done.6
  259.6 3.4 multiply_convert_fusion
  263.0 0.4 copy-done.2
  263.4 2.7 fusion.19
  266.1 7.9 %fusion.3 = f32[768,6144]{1,0:T(8,128)} fusion(bf16[768,256]{1,0:T(8,128)(2,1)S(1)} %bitcast.79, bf16[1,6144,256]{2,1,0:T(8,128)(2,1)S(1)} %copy-done), kind=kOutput, calls=%fused_computation.4 | convolution fusion | flops 2415919104 | bytes 22413312 | tf_op jit(solution)/shard_map/dot_general | solution.py:66
  274.0 13.8 %fusion = bf16[6144,768]{0,1:T(8,128)(2,1)} fusion(f32[768,6144]{1,0:T(8,128)} %fusion.3, bf16[768,256]{1,0:T(8,128)(2,1)} %bitcast.77, bf16[1,6144,256]{2,1,0:T(8,128)(2,1)} %param.12), kind=kOutput, calls=%fused_computation.1 | convolution fusion | flops 2425356288 | bytes 31850496 | tf_op jit(solution)/shard_map/dot_general | solution.py:66
  287.9 102.7 %reduce-scatter.5.cloned.1.call-done = bf16[768,768]{0,1:T(8,128)(2,1)} async-done(((bf16[6144,768]{0,1:T(8,128)(2,1)}), bf16[768,768]{0,1:T(8,128)(2,1)}) %reduce-scatter.5.cloned.1.call-update) | async-done | bytes 1179664 | tf_op jit(solution)/shard_map/reduce_scatter | solution.py:50
  390.6 2.4 copy.109
  393.0 24.0 %reduce-scatter.7.cloned.1.call-done = bf16[192,768]{1,0:T(8,128)(2,1)} async-done(((bf16[768,768]{1,0:T(8,128)(2,1)}), bf16[192,768]{1,0:T(8,128)(2,1)}) %reduce-scatter.7.cloned.1.call-update) | async-done | bytes 294928
  417.0 1.9 copy.110
  418.9 1.4 copy.99
  420.3 14.5 %all_to_all.27 = bf16[192,2,384]{0,1,2:T(2,128)(2,1)S(1)} all-to-all(bf16[192,2,384]{0,1,2:T(2,128)(2,1)S(1)} %copy.99), channel_id=1, replica_groups=mesh['pipe_0'=8,'pipe_1'=4,'expert'=8] {'expert'}, dimensions={2} | all-to-all | bytes 589824 | tf_op jit(solution)/shard_map/all_to_all | solution.py:126
  434.8 1.1 fusion.22
  435.9 2.0 copy.101
  437.8 1.4 bitcast_reduce_fusion
  439.3 2.1 fusion.36
  441.4 0.6 broadcast_in_dim.11
  441.9 4.1 all-to-all-start.4
  446.0 1.5 copy.103
  447.5 3.2 all-to-all-done.4
  450.6 1.3 broadcast_in_dim.10
  451.9 8.1 %all-to-all-start.3 = ((f32[32,2,128]{2,1,0:T(2,128)}), f32[32,2,128]{2,1,0:T(2,128)}, u32[]{:S(2)}, u32[]{:S(2)}) async-start(f32[32,2,128]{2,1,0:T(2,128)} %broadcast_in_dim.10), calls=%async_computation.4 | async-start | bytes 65536 | tf_op jit(solution)/shard_map/all_to_all | solution.py:13
  460.1 0.7 copy.102
  460.8 0.6 reduce_sum.79
  461.4 7.3 %all-to-all-done.3 = f32[32,2,128]{2,1,0:T(2,128)} async-done(((f32[32,2,128]{2,1,0:T(2,128)}), f32[32,2,128]{2,1,0:T(2,128)}, u32[]{:S(2)}, u32[]{:S(2)}) %all-to-all-start.3) | async-done | bytes 32800 | tf_op jit(solution)/shard_map/all_to_all | solution.py:13
  468.7 0.8 reduce_sum.77
  469.5 0.7 copy.105
  470.2 2.2 fusion.33
  472.4 1.8 copy.107
  (32 shorter events, 0.5 us)
Async XLA Ops:
  7.2 245.1 %copy-start = (bf16[1,6144,256]{2,1,0:T(8,128)(2,1)S(1)}, bf16[1,6144,256]{2,1,0:T(8,128)(2,1)}, u32[]{:S(2)}) copy-start(bf16[1,6144,256]{2,1,0:T(8,128)(2,1)} %param.11) | copy-start | bytes 9437188
  9.3 20.8 %all-to-all-start = ((f32[32,2,128]{2,1,0:T(2,128)}), f32[32,2,128]{2,1,0:T(2,128)}, u32[]{:S(2)}, u32[]{:S(2)}) async-start(f32[32,2,128]{2,1,0:T(2,128)} %broadcast_in_dim.8), calls=%async_computation | async-start | bytes 65536 | tf_op jit(solution)/shard_map/all_to_all | solution.py:13
  21.4 190.8 %all-gather.2.cloned.1.call-start = ((), (), s32[]{:S(2)}) async-start(), calls=%async_computation.7 | async-start | bytes 19464192 | tf_op jit(solution)/shard_map/all_gather | solution.py:39
  25.2 201.6 %copy-start.3 = (bf16[2,128,192]{2,0,1:T(2,128)(2,1)}, bf16[2,128,192]{2,0,1:T(2,128)(2,1)S(1)}, u32[]{:S(2)}) copy-start(bf16[2,128,192]{2,0,1:T(2,128)(2,1)S(1)} %copy.83) | copy-start | bytes 294916
  31.1 195.8 %copy-start.4 = (f32[2,128]{0,1:T(8,128)}, f32[2,128]{0,1:T(8,128)S(1)}, u32[]{:S(2)}) copy-start(f32[2,128]{0,1:T(8,128)S(1)} %copy.87) | copy-start | bytes 3076
  65.0 325.6 %reduce-scatter.5.cloned.1.call-start = ((), (), s32[]{:S(2)}) async-start(), calls=%async_computation.8 | async-start | bytes 10616832 | tf_op jit(solution)/shard_map/reduce_scatter | solution.py:50
  252.2 6.4 %copy-start.1 = (bf16[6144,768]{0,1:T(8,128)(2,1)S(1)}, bf16[6144,768]{0,1:T(8,128)(2,1)}, u32[]{:S(2)}) copy-start(bf16[6144,768]{0,1:T(8,128)(2,1)} %copy.97) | copy-start | bytes 28311556
  252.2 7.3 %copy-start.6 = (bf16[1,256,6144]{2,1,0:T(8,128)(2,1)S(1)}, bf16[1,256,6144]{2,1,0:T(8,128)(2,1)}, u32[]{:S(2)}) copy-start(bf16[1,256,6144]{2,1,0:T(8,128)(2,1)} %param.13) | copy-start | bytes 9437188
  252.2 10.7 %slice-start = ((s8[9437184]{0:T(1024)(128)(4,1)}), s8[4194304]{0:T(1024)(128)(4,1)S(1)}, s32[]{:S(2)}) async-start(s8[9437184]{0:T(1024)(128)(4,1)} %bitcast.68), calls=%async_computation.10 | async-start | bytes 8388608
  252.3 10.7 %slice-start.1 = ((s8[9437184]{0:T(1024)(128)(4,1)}), s8[4194304]{0:T(1024)(128)(4,1)S(1)}, s32[]{:S(2)}) async-start(s8[9437184]{0:T(1024)(128)(4,1)} %bitcast.68), calls=%async_computation.11 | async-start | bytes 8388608
  259.6 3.4 slice-start.2
  259.6 3.8 copy-start.2
  287.8 151.5 %copy-start.5 = (f32[192]{0:T(256)S(1)}, f32[192]{0:T(256)}, u32[]{:S(2)}) copy-start(f32[192]{0:T(256)} %param.10) | copy-start | bytes 2308
  287.8 129.2 %reduce-scatter.7.cloned.1.call-start = ((), (), s32[]{:S(2)}) async-start(), calls=%async_computation.9 | async-start | bytes 1474560
  441.9 8.7 %all-to-all-start.4 = ((f32[8,1,192]{2,1,0:T(1,128)}), f32[8,1,192]{2,1,0:T(1,128)S(1)}, u32[]{:S(2)}, u32[]{:S(2)}) async-start(f32[8,1,192]{2,1,0:T(1,128)} %broadcast_in_dim.11), calls=%async_computation.5 | async-start | bytes 16384 | tf_op jit(solution)/shard_map/all_to_all | solution.py:13
  451.9 16.7 %all-to-all-start.3 = ((f32[32,2,128]{2,1,0:T(2,128)}), f32[32,2,128]{2,1,0:T(2,128)}, u32[]{:S(2)}, u32[]{:S(2)}) async-start(f32[32,2,128]{2,1,0:T(2,128)} %broadcast_in_dim.10), calls=%async_computation.4 | async-start | bytes 65536 | tf_op jit(solution)/shard_map/all_to_all | solution.py:13
Sparse Core Ops, SparseCore 0:
  65.1 147.1 all-gather.1
  288.0 102.5 reduce-scatter.4
  393.1 23.8 reduce-scatter.6
where the time goes:
time: 482 us; the launch traced here: 481 us
  waiting for transfers between devices  285 us (59%)
  local copies, waits for them, and re-layouts  72.2 us (15%)
  matrix products  35.6 us (7%)
  blocking collectives  33 us (7%)
  starting transfers between devices  24.6 us (5%)
  other arithmetic  16 us (3%)
  between operations  13.9 us (3%)
    all_gather x1, waiting for transfers between devices, rows_first(): out, at, gathered = (lax.all_gather(both, axis, axis=0, tiled=True), 0, [])  147 us
    reduce_scatter x1, waiting for transfers between devices, sum_by_axis(): total = lax.psum_scatter(total, axis, scatter_dimension=0, tiled=True)  103 us
    slice x3, local copies, waits for them, and re-layouts, rows_first(): section = out[:, at:at + t[0].size].reshape(-1, *t.shape[1:])  40 us
    all_to_all x3, starting transfers between devices, from_everyone(): lax.all_to_all(jnp.broadcast_to(x[None], (devices, *x.shape)), axis, 0, 0...  24.3 us
    unnamed x4, waiting for transfers between devices  24.1 us
    dot_general x2, matrix products, contract_last(): lax.dot_general(left, right, (((1,), (1,)), ((), ())), preferred_element_...  21.7 us
    all_to_all x1, blocking collectives, in_one_piece(): lax.all_to_all(both, axis, split_axis=split_dim, concat_axis=concat_dim,...  18.5 us
    all_to_all x1, blocking collectives, body(): lax.all_to_all(d_rows, 'expert', split_axis=2, concat_axis=2, tiled=True)  14.5 us
  transfers between devices with their start and end apart: 6, of which 6 were waited for; matrix products, arithmetic and copies ran while one was open for 2% of the time, Pallas kernels for 0%

commit v1 on v0

--- a/solution.py
+++ b/solution.py
@@ -36,7 +36,17 @@
 def rows_first(arrays, axis, dims):
     turned = [jnp.moveaxis(a, dim, 0) for a, dim in zip(arrays, dims)]
     both = jnp.concatenate([t.reshape(len(t), -1) for t in turned], axis=1)
-    out, at, gathered = (lax.all_gather(both, axis, axis=0, tiled=True), 0, [])
+
+    def spots_feed(shard_axis, x_in):
+        y1 = lax.all_to_all(
+            jnp.stack([x_in for _ in range(lax.psum(1, shard_axis))], axis=0),
+            axis_name=shard_axis,
+            split_axis=0,
+            concat_axis=0,
+        )
+        return jnp.concatenate(y1, axis=0)
+
+    out, at, gathered = (spots_feed(axis, both), 0, [])
     for t, dim in zip(turned, dims):
         section = out[:, at : at + t[0].size].reshape(-1, *t.shape[1:])
         gathered.append(jnp.moveaxis(section, 0, dim))

time: 482 us -> 749 us (1.55)
  blocking collectives: 33 us -> 448 us
  waiting for transfers between devices: 285 us -> 138 us
    all_to_all x0 -> x1, blocking collectives: none -> 415 us  [spots_feed(): lax.all_to_all(jnp.stack([x_in for _ in range(lax.psum(1, shard_axis))],...]
    all_gather x1 -> x0, waiting for transfers between devices: 147 us -> none  [rows_first(): out, at, gathered = (lax.all_gather(both, axis, axis=0, tiled=True), 0, [])]
    slice x3, local copies, waits for them, and re-layouts: 40 us -> 32 us  [rows_first(): section = out[:, at:at + t[0].size].reshape(-1, *t.shape[1:])]
    unnamed x4 -> x3, waiting for transfers between devices: 24.1 us -> 24.2 us
  transfers between devices with their start and end apart: 6 -> 5, of which waited for: 6 -> 5; matrix products, arithmetic and copies ran while one was open for 2% -> 1% of each run, Pallas kernels for 0% -> 0%
where the time goes in v1:
time: 749 us; the launch traced here: 747 us
  blocking collectives  448 us (60%)
  waiting for transfers between devices  138 us (18%)
  local copies, waits for them, and re-layouts  71.1 us (9%)
  matrix products  35.6 us (5%)
  starting transfers between devices  24.4 us (3%)
  other arithmetic  15.2 us (2%)
  between operations  14.2 us (2%)
    all_to_all x1, blocking collectives, spots_feed(): lax.all_to_all(jnp.stack([x_in for _ in range(lax.psum(1, shard_axis))],...  415 us
    reduce_scatter x1, waiting for transfers between devices, sum_by_axis(): total = lax.psum_scatter(total, axis, scatter_dimension=0, tiled=True)  103 us
    slice x3, local copies, waits for them, and re-layouts, rows_first(): section = out[:, at:at + t[0].size].reshape(-1, *t.shape[1:])  32 us
    all_to_all x3, starting transfers between devices, from_everyone(): lax.all_to_all(jnp.broadcast_to(x[None], (devices, *x.shape)), axis, 0, 0...  24.4 us
    unnamed x3, waiting for transfers between devices  24.2 us
    dot_general x2, matrix products, contract_last(): lax.dot_general(left, right, (((1,), (1,)), ((), ())), preferred_element_...  21.7 us
    all_to_all x1, blocking collectives, in_one_piece(): lax.all_to_all(both, axis, split_axis=split_dim, concat_axis=concat_dim,...  18.5 us
  transfers between devices with their start and end apart: 5, of which 5 were waited for; matrix products, arithmetic and copies ran while one was open for 1% of the time, Pallas kernels for 0%

profile of v1, /device:TPU:1, one launch (start us, length us, event | category | flops | bytes accessed | tf_op | source)
XLA Modules:
  0.0 746.7 jit_solution(13980217614582786998)
XLA Ops:
  7.2 1.2 copy.84
  8.4 0.2 fusion.28
  8.6 0.6 broadcast_in_dim.8
  9.3 12.2 %all-to-all-start = ((f32[32,2,128]{2,1,0:T(2,128)}), f32[32,2,128]{2,1,0:T(2,128)}, u32[]{:S(2)}, u32[]{:S(2)}) async-start(f32[32,2,128]{2,1,0:T(2,128)} %broadcast_in_dim.8), calls=%async_computation | async-start | bytes 65536 | tf_op jit(solution)/shard_map/all_to_all | solution.py:13
  21.5 0.8 copy.88
  22.3 0.1 eq.39
  22.5 0.1 reshape.89
  22.6 1.2 reduce-window.6
  23.8 0.2 slice_reduce_fusion
  24.1 1.0 copy.83
  25.2 0.8 convert_element_type.40
  26.0 0.8 copy.108
  26.8 1.3 fusion.23
  28.1 1.1 convolution_convert_fusion
  29.1 1.0 all-to-all-done
  30.1 0.8 reduce_sum.73
  31.1 0.9 fusion.30
  32.0 0.1 broadcast_in_dim.9
  32.1 0.3 convolution_convert_fusion.1
  32.5 1.8 pad_maximum_fusion
  34.3 2.2 copy.94
  36.5 18.5 %all_to_all.31 = bf16[4,384,192]{2,0,1:T(4,128)(2,1)S(1)} all-to-all(bf16[4,384,192]{2,0,1:T(4,128)(2,1)} %copy.94), channel_id=1, replica_groups=mesh['pipe_0'=8,'pipe_1'=4,'expert'=8] {'expert'}, dimensions={1} | all-to-all | bytes 1179648 | tf_op jit(solution)/shard_map/all_to_all | solution.py:29
  55.0 1.4 slice_bitcast_fusion.1
  56.5 2.0 copy.95
  58.5 1.7 copy.115
  60.2 2.0 copy.96
  62.2 1.0 copy.116
  63.1 1.0 pad_maximum_fusion.1
  64.2 6.7 stack.2
  70.9 415.2 %all_to_all.32 = bf16[32,192,1536]{2,1,0:T(8,128)(2,1)S(1)} all-to-all(bf16[32,192,1536]{2,1,0:T(8,128)(2,1)} %stack.2), channel_id=1, replica_groups=mesh['pipe_0'=8,'pipe_1'=4,'expert'=8] {'pipe_0','pipe_1'}, dimensions={0} | all-to-all | bytes 37748736 | tf_op jit(solution)/shard_map/all_to_all | solution.py:41
  486.0 6.6 fusion.42
  492.6 12.7 %copy.98 = bf16[6144,768]{0,1:T(8,128)(2,1)} copy(bf16[6144,768]{1,0:T(8,128)(2,1)} %get-tuple-element.12) | data formatting | bytes 18874368 | tf_op jit(solution)/shard_map/slice | solution.py:51
  505.3 12.7 %copy.97 = bf16[6144,768]{0,1:T(8,128)(2,1)} copy(bf16[6144,768]{1,0:T(8,128)(2,1)} %get-tuple-element.13) | data formatting | bytes 18874368 | tf_op jit(solution)/shard_map/slice | solution.py:51
  518.0 5.3 fusion.1
  523.4 1.1 copy-done.1
  524.5 0.9 copy-done.6
  525.4 3.4 multiply_convert_fusion
  528.8 0.5 copy-done.2
  529.3 2.7 fusion.19
  532.0 7.9 %fusion.3 = f32[768,6144]{1,0:T(8,128)} fusion(bf16[768,256]{1,0:T(8,128)(2,1)S(1)} %bitcast.81, bf16[1,6144,256]{2,1,0:T(8,128)(2,1)S(1)} %copy-done), kind=kOutput, calls=%fused_computation.4 | convolution fusion | flops 2415919104 | bytes 22413312 | tf_op jit(solution)/shard_map/dot_general | solution.py:76
  539.9 13.8 %fusion = bf16[6144,768]{0,1:T(8,128)(2,1)} fusion(f32[768,6144]{1,0:T(8,128)} %fusion.3, bf16[768,256]{1,0:T(8,128)(2,1)} %bitcast.79, bf16[1,6144,256]{2,1,0:T(8,128)(2,1)} %param.12), kind=kOutput, calls=%fused_computation.1 | convolution fusion | flops 2425356288 | bytes 31850496 | tf_op jit(solution)/shard_map/dot_general | solution.py:76
  553.8 102.6 %reduce-scatter.5.cloned.1.call-done = bf16[768,768]{0,1:T(8,128)(2,1)} async-done(((bf16[6144,768]{0,1:T(8,128)(2,1)}), bf16[768,768]{0,1:T(8,128)(2,1)}) %reduce-scatter.5.cloned.1.call-update) | async-done | bytes 1179664 | tf_op jit(solution)/shard_map/reduce_scatter | solution.py:60
  656.3 2.4 copy.109
  658.8 24.1 %reduce-scatter.7.cloned.1.call-done = bf16[192,768]{1,0:T(8,128)(2,1)} async-done(((bf16[768,768]{1,0:T(8,128)(2,1)}), bf16[192,768]{1,0:T(8,128)(2,1)}) %reduce-scatter.7.cloned.1.call-update) | async-done | bytes 294928
  682.9 1.9 copy.110
  684.8 1.4 copy.99
  686.2 14.3 %all_to_all.33 = bf16[192,2,384]{0,1,2:T(2,128)(2,1)S(1)} all-to-all(bf16[192,2,384]{0,1,2:T(2,128)(2,1)S(1)} %copy.99), channel_id=1, replica_groups=mesh['pipe_0'=8,'pipe_1'=4,'expert'=8] {'expert'}, dimensions={2} | all-to-all | bytes 589824 | tf_op jit(solution)/shard_map/all_to_all | solution.py:136
  700.4 1.1 fusion.22
  701.5 2.0 copy.101
  703.5 1.4 bitcast_reduce_fusion
  705.0 2.1 fusion.36
  707.0 0.6 broadcast_in_dim.11
  707.6 4.1 all-to-all-start.5
  711.7 1.5 copy.103
  713.2 3.2 all-to-all-done.5
  716.3 1.3 broadcast_in_dim.10
  717.6 8.2 %all-to-all-start.4 = ((f32[32,2,128]{2,1,0:T(2,128)}), f32[32,2,128]{2,1,0:T(2,128)}, u32[]{:S(2)}, u32[]{:S(2)}) async-start(f32[32,2,128]{2,1,0:T(2,128)} %broadcast_in_dim.10), calls=%async_computation.5 | async-start | bytes 65536 | tf_op jit(solution)/shard_map/all_to_all | solution.py:13
  725.8 0.7 copy.102
  726.5 0.6 reduce_sum.79
  727.1 7.3 all-to-all-done.4
  734.4 0.8 reduce_sum.77
  735.2 0.7 copy.105
  736.0 2.2 fusion.33
  738.1 1.8 copy.107
  (31 shorter events, 0.5 us)
Async XLA Ops:
  7.2 510.9 %copy-start = (bf16[1,6144,256]{2,1,0:T(8,128)(2,1)S(1)}, bf16[1,6144,256]{2,1,0:T(8,128)(2,1)}, u32[]{:S(2)}) copy-start(bf16[1,6144,256]{2,1,0:T(8,128)(2,1)} %param.11) | copy-start | bytes 9437188
  9.3 20.8 %all-to-all-start = ((f32[32,2,128]{2,1,0:T(2,128)}), f32[32,2,128]{2,1,0:T(2,128)}, u32[]{:S(2)}, u32[]{:S(2)}) async-start(f32[32,2,128]{2,1,0:T(2,128)} %broadcast_in_dim.8), calls=%async_computation | async-start | bytes 65536 | tf_op jit(solution)/shard_map/all_to_all | solution.py:13
  21.4 634.9 %reduce-scatter.5.cloned.1.call-start = ((), (), s32[]{:S(2)}) async-start(), calls=%async_computation.8 | async-start | bytes 10616832 | tf_op jit(solution)/shard_map/reduce_scatter | solution.py:60
  25.2 45.7 %copy-start.3 = (bf16[2,128,192]{2,0,1:T(2,128)(2,1)}, bf16[2,128,192]{2,0,1:T(2,128)(2,1)S(1)}, u32[]{:S(2)}) copy-start(bf16[2,128,192]{2,0,1:T(2,128)(2,1)S(1)} %copy.83) | copy-start | bytes 294916
  31.1 39.8 %copy-start.4 = (f32[2,128]{0,1:T(8,128)}, f32[2,128]{0,1:T(8,128)S(1)}, u32[]{:S(2)}) copy-start(f32[2,128]{0,1:T(8,128)S(1)} %copy.87) | copy-start | bytes 3076
  518.0 6.4 copy-start.1
  518.0 7.3 copy-start.6
  518.0 10.7 %slice-start = ((s8[9437184]{0:T(1024)(128)(4,1)}), s8[4194304]{0:T(1024)(128)(4,1)S(1)}, s32[]{:S(2)}) async-start(s8[9437184]{0:T(1024)(128)(4,1)} %bitcast.70), calls=%async_computation.10 | async-start | bytes 8388608
  518.0 10.7 %slice-start.1 = ((s8[9437184]{0:T(1024)(128)(4,1)}), s8[4194304]{0:T(1024)(128)(4,1)S(1)}, s32[]{:S(2)}) async-start(s8[9437184]{0:T(1024)(128)(4,1)} %bitcast.70), calls=%async_computation.11 | async-start | bytes 8388608
  525.3 3.4 slice-start.2
  525.4 3.9 copy-start.2
  553.7 151.3 %copy-start.5 = (f32[192]{0:T(256)S(1)}, f32[192]{0:T(256)}, u32[]{:S(2)}) copy-start(f32[192]{0:T(256)} %param.10) | copy-start | bytes 2308
  553.7 129.2 %reduce-scatter.7.cloned.1.call-start = ((), (), s32[]{:S(2)}) async-start(), calls=%async_computation.9 | async-start | bytes 1474560
  707.6 8.7 %all-to-all-start.5 = ((f32[8,1,192]{2,1,0:T(1,128)}), f32[8,1,192]{2,1,0:T(1,128)S(1)}, u32[]{:S(2)}, u32[]{:S(2)}) async-start(f32[8,1,192]{2,1,0:T(1,128)} %broadcast_in_dim.11), calls=%async_computation.6 | async-start | bytes 16384 | tf_op jit(solution)/shard_map/all_to_all | solution.py:13
  717.6 16.8 %all-to-all-start.4 = ((f32[32,2,128]{2,1,0:T(2,128)}), f32[32,2,128]{2,1,0:T(2,128)}, u32[]{:S(2)}, u32[]{:S(2)}) async-start(f32[32,2,128]{2,1,0:T(2,128)} %broadcast_in_dim.10), calls=%async_computation.5 | async-start | bytes 65536 | tf_op jit(solution)/shard_map/all_to_all | solution.py:13
Sparse Core Ops, SparseCore 0:
  553.8 102.4 reduce-scatter.4
  658.9 23.9 reduce-scatter.6
